TPU v7x, 256 devices: a whole 4x4x8 slice. The times are simulated.
256 devices in a mesh: rows: 64 (over z, x, core), coil: 4 (over y).
Axes of the slice: x: 4, y: 4, z: 8, core: 2. Of those that a mesh axis runs over, the one named last changes fastest.
Arguments:
- kspace: float32 [128, 32768], P('coil', 'rows'), may hold values from -6 to 6
- sample_mask: int32 [128, 32768], P('coil', 'rows'), may hold values 0 or 1
- start_basis: float32 [4, 2048, 128], P('coil', 'rows'), may hold values from -6 to 6
Outputs:
- recovered: float32 [128, 32768], P('coil', 'rows')
- basis: float32 [4, 2048, 128], P('coil', 'rows')
All inputs are finite; a program needn't handle non-finite values. No bound on the sum of `sample_mask` on one device may be relied on, other than what follows from the above.
Results may differ from a plain program's by a relative error of at most 0.00011.
Values sent between devices are 32-bit elements; how exact they have to be, the bound alone decides.
A program may use at most 64 MiB of HBM per device.

v0:
```python
import jax
import jax.numpy as jnp
from jax import lax
from jax.sharding import PartitionSpec as P

KER = 64
ITERS = 2
threshold = 0.05


def shifted(block, axis, distance):
    devices = range(lax.axis_size(axis))
    route = [((i - distance) % len(devices), i) for i in devices]
    return lax.ppermute(block, axis, route)


def orthonormal(normal_rows, gram_matrix):
    factor = jnp.linalg.cholesky(gram_matrix)
    return lax.linalg.triangular_solve(
        factor, normal_rows, left_side=False, lower=True, transpose_a=True
    )


def coil_total(partial_value):
    return lax.psum(partial_value, "coil")


def shards(kspace, sample_mask, start_basis):
    highest = lax.Precision.HIGHEST
    channels = kspace.shape[0]
    tile_rows = kspace.shape[1]
    mask_float = sample_mask.astype(jnp.float32)
    sampled = kspace * mask_float
    next_rim = shifted(sampled[:, : KER - 1], "rows", -1)
    extended = jnp.concatenate([sampled, next_rim], axis=1)
    hankel_cols = jnp.stack(
        [extended[:, offset : offset + tile_rows] for offset in range(KER)], axis=0
    )
    hankel_cols = hankel_cols.reshape(KER * channels, tile_rows)
    owned_basis = start_basis.reshape(start_basis.shape[1], start_basis.shape[2])

    def fold_basis(shard_piece):
        return lax.dot_general(
            shard_piece,
            hankel_cols,
            (((0,), (0,)), ((), ())),
            precision=highest,
            preferred_element_type=jnp.float32,
        )

    def apply_hankel(current):
        partial_value = fold_basis(lax.all_gather(current, "rows", axis=0, tiled=True))
        return coil_total(partial_value)

    for iteration in range(ITERS):
        images = apply_hankel(owned_basis)
        normal_rows = lax.psum_scatter(
            lax.dot_general(
                hankel_cols,
                images,
                (((1,), (1,)), ((), ())),
                precision=highest,
                preferred_element_type=jnp.float32,
            ),
            "rows",
            scatter_dimension=0,
            tiled=True,
        )
        local_gram = jnp.dot(
            normal_rows.T, normal_rows, precision=highest, preferred_element_type=jnp.float32
        )
        gram_matrix = lax.psum(local_gram, ("rows", "coil"))
        owned_basis = orthonormal(normal_rows, gram_matrix)
    images = apply_hankel(owned_basis)
    projected = jnp.dot(
        lax.all_gather(owned_basis, "rows", axis=0, tiled=True),
        images,
        precision=highest,
        preferred_element_type=jnp.float32,
    )
    stacked = projected.reshape(KER, channels, tile_rows)
    spread = jnp.zeros((channels, tile_rows + KER - 1), jnp.float32)
    for offset in range(KER):
        spread = spread.at[:, offset : offset + tile_rows].add(stacked[offset])
    carried = shifted(spread[:, tile_rows:], "rows", 1)
    estimate = spread[:, :tile_rows].at[:, : KER - 1].add(carried) / KER
    residual = mask_float * (kspace - estimate)
    recovered = estimate + residual - jnp.clip(residual, -threshold, threshold)
    return (recovered, owned_basis.reshape(1, owned_basis.shape[0], owned_basis.shape[1]))


def solution(mesh):
    return jax.shard_map(
        shards,
        mesh=mesh,
        in_specs=(P("coil", "rows"), P("coil", "rows"), P("coil", "rows", None)),
        out_specs=(P("coil", "rows"), P("coil", "rows", None)),
        check_vma=False,
    )
```

profile of v0, /device:TPU:16, one launch (start us, length us, event | category | flops | bytes accessed | tf_op | source)
XLA Modules:
  0.0 1392.1 jit_solution(3663720347566413571)
XLA Ops:
  8.7 7.5 collective-permute-start
  62.2 28.1 %all-gather.9.cloned.1.call-done = f32[1,2048,128]{2,1,0:T(8,128)} async-done(((f32[1,32,128]{2,1,0:T(8,128)}), f32[1,2048,128]{2,1,0:T(8,128)}) %all-gather.9.cloned.1.call-update) | async-done | bytes 1048592 | tf_op jit(solution)/shard_map/all_gather | solution.py:52
  90.4 9.9 convolution_bitcast_fusion
  100.5 43.9 %all-reduce.7.cloned.1.call-done = f32[128,512]{0,1:T(8,128)} async-done(((f32[128,512]{0,1:T(8,128)}), f32[128,512]{0,1:T(8,128)}) %all-reduce.7.cloned.1.call-update) | async-done | bytes 262160 | tf_op jit(solution)/shard_map/psum | solution.py:25
  144.4 6.6 fusion.135
  151.0 141.7 %reduce-scatter.3.cloned.1.call-done = f32[32,128]{1,0:T(8,128)} async-done(((f32[2048,128]{1,0:T(8,128)}), f32[32,128]{1,0:T(8,128)}) %reduce-scatter.3.cloned.1.call-update) | async-done | bytes 16400 | tf_op jit(solution)/shard_map/reduce_scatter | solution.py:57
  292.7 1.7 fusion.136
  294.5 243.0 %all-reduce.9.cloned.1.call-done = f32[128,128]{0,1:T(8,128)} async-done(((f32[128,128]{0,1:T(8,128)}), f32[128,128]{0,1:T(8,128)}) %all-reduce.9.cloned.1.call-update) | async-done | bytes 65552 | tf_op jit(solution)/shard_map/psum | solution.py:72
  539.3 11.7 cholesky.44
  552.3 9.8 custom-call.6
  563.9 74.0 %all-gather.5.cloned.1.call-done = f32[2048,128]{1,0:T(8,128)} async-done(((f32[32,128]{1,0:T(8,128)}), f32[2048,128]{1,0:T(8,128)}) %all-gather.5.cloned.1.call-update) | async-done | bytes 1048592 | tf_op jit(solution)/shard_map/all_gather | solution.py:52
  637.9 5.8 fusion.137
  643.8 44.0 %all-reduce.11.cloned.1.call-done = f32[128,512]{1,0:T(8,128)} async-done(((f32[128,512]{1,0:T(8,128)}), f32[128,512]{1,0:T(8,128)}) %all-reduce.11.cloned.1.call-update) | async-done | bytes 262160 | tf_op jit(solution)/shard_map/psum | solution.py:25
  687.9 6.6 fusion.138
  694.6 141.7 %reduce-scatter.5.cloned.1.call-done = f32[32,128]{1,0:T(8,128)} async-done(((f32[2048,128]{1,0:T(8,128)}), f32[32,128]{1,0:T(8,128)}) %reduce-scatter.5.cloned.1.call-update) | async-done | bytes 16400 | tf_op jit(solution)/shard_map/reduce_scatter | solution.py:57
  836.3 1.7 fusion.139
  838.5 242.7 %all-reduce.13.cloned.1.call-done = f32[128,128]{0,1:T(8,128)} async-done(((f32[128,128]{0,1:T(8,128)}), f32[128,128]{0,1:T(8,128)}) %all-reduce.13.cloned.1.call-update) | async-done | bytes 65552 | tf_op jit(solution)/shard_map/psum | solution.py:72
  1083.0 11.7 cholesky.55
  1096.0 9.8 custom-call.7
  1107.4 74.2 %all-gather.7.cloned.1.call-done = f32[2048,128]{1,0:T(8,128)} async-done(((f32[32,128]{1,0:T(8,128)}), f32[2048,128]{1,0:T(8,128)}) %all-gather.7.cloned.1.call-update) | async-done | bytes 1048592 | tf_op jit(solution)/shard_map/all_gather | solution.py:76
  1181.6 5.9 fusion.140
  1230.1 1.6 all-reduce.15.cloned.1.call-done
  1231.7 4.5 fusion.141
  1241.0 1.6 add_select_fusion.59
  1243.2 1.6 add_select_fusion.58
  1252.1 1.6 add_select_fusion.54
  1256.6 1.6 add_select_fusion.52
  1258.9 1.5 add_select_fusion.51
  1261.1 1.6 add_select_fusion.50
  1263.4 1.5 add_select_fusion.49
  1265.6 1.6 add_select_fusion.48
  1270.0 1.6 add_select_fusion.46
  1272.3 1.5 add_select_fusion.45
  1274.5 1.6 add_select_fusion.44
  1279.1 1.6 add_select_fusion.42
  1281.4 1.6 add_select_fusion.41
  1285.9 1.5 add_select_fusion.39
  1288.2 1.5 add_select_fusion.38
  1290.4 1.5 add_select_fusion.37
  1292.6 1.5 add_select_fusion.36
  1294.9 1.6 add_select_fusion.35
  1299.4 1.6 add_select_fusion.33
  1301.7 1.6 add_select_fusion.32
  1304.0 1.6 add_select_fusion.31
  1308.4 1.6 add_select_fusion.29
  1312.9 1.6 add_select_fusion.27
  1319.6 1.6 add_select_fusion.24
  1321.9 1.6 add_select_fusion.23
  1326.4 1.5 add_select_fusion.21
  1328.6 1.5 add_select_fusion.20
  1330.9 1.6 add_select_fusion.19
  1335.3 1.6 add_select_fusion.17
  1339.8 1.6 add_select_fusion.15
  1344.2 1.6 add_select_fusion.13
  1348.7 1.6 add_select_fusion.11
  1350.9 1.5 add_select_fusion.10
  1353.1 1.6 add_select_fusion.9
  1355.4 1.5 add_select_fusion.8
  1359.8 1.6 add_select_fusion.6
  1364.3 1.6 add_select_fusion.4
  1366.6 1.5 add_select_fusion.3
  1369.1 1.6 add_select_fusion.2
  1371.3 1.6 add_select_fusion.1
  1378.1 5.2 collective-permute-done.1
  (264 shorter events, 180.3 us)
Async XLA Ops:
  7.2 83.2 %all-gather.9.cloned.1.call-start = ((), (), s32[]{:S(2)}) async-start(), calls=%async_computation.11 | async-start | bytes 1064960 | tf_op jit(solution)/shard_map/all_gather | solution.py:52
  8.7 8.9 collective-permute-start
  16.2 128.1 %all-reduce.7.cloned.1.call-start = ((), (), s32[]{:S(2)}) async-start(), calls=%async_computation.2 | async-start | bytes 524288 | tf_op jit(solution)/shard_map/psum | solution.py:25
  100.3 192.4 %reduce-scatter.3.cloned.1.call-start = ((), (), s32[]{:S(2)}) async-start(), calls=%async_computation.3 | async-start | bytes 1064960 | tf_op jit(solution)/shard_map/reduce_scatter | solution.py:57
  151.0 386.5 %all-reduce.9.cloned.1.call-start = ((), (), s32[]{:S(2)}) async-start(), calls=%async_computation.4 | async-start | bytes 131072 | tf_op jit(solution)/shard_map/psum | solution.py:72
  294.4 343.5 %all-gather.5.cloned.1.call-start = ((), (), s32[]{:S(2)}) async-start(), calls=%async_computation.5 | async-start | bytes 1064960 | tf_op jit(solution)/shard_map/all_gather | solution.py:52
  563.7 124.2 %all-reduce.11.cloned.1.call-start = ((), (), s32[]{:S(2)}) async-start(), calls=%async_computation.6 | async-start | bytes 524288 | tf_op jit(solution)/shard_map/psum | solution.py:25
  643.8 192.5 %reduce-scatter.5.cloned.1.call-start = ((), (), s32[]{:S(2)}) async-start(), calls=%async_computation.7 | async-start | bytes 1064960 | tf_op jit(solution)/shard_map/reduce_scatter | solution.py:57
  694.5 386.7 %all-reduce.13.cloned.1.call-start = ((), (), s32[]{:S(2)}) async-start(), calls=%async_computation.8 | async-start | bytes 131072 | tf_op jit(solution)/shard_map/psum | solution.py:72
  838.0 343.6 %all-gather.7.cloned.1.call-start = ((), (), s32[]{:S(2)}) async-start(), calls=%async_computation.9 | async-start | bytes 1064960 | tf_op jit(solution)/shard_map/all_gather | solution.py:76
  1107.4 124.3 %all-reduce.15.cloned.1.call-start = ((), (), s32[]{:S(2)}) async-start(), calls=%async_computation.10 | async-start | bytes 524288 | tf_op jit(solution)/shard_map/psum | solution.py:25
  1181.6 50.0 %copy-start.1 = (f32[2048,128]{1,0:T(8,128)S(1)}, f32[2048,128]{1,0:T(8,128)}, u32[]{:S(2)}) copy-start(f32[2048,128]{1,0:T(8,128)} %all-gather.7.cloned.1.call-done) | copy-start | bytes 3145732
  1236.1 2.0 copy-start
  1321.9 62.4 %copy-start.2 = (f32[32,512]{1,0:T(8,128)S(1)}, f32[32,512]{1,0:T(8,128)}, u32[]{:S(2)}) copy-start(f32[32,512]{1,0:T(8,128)} %param.136) | copy-start | bytes 196612
  1321.9 62.4 %copy-start.3 = (s32[32,512]{1,0:T(8,128)S(1)}, s32[32,512]{1,0:T(8,128)}, u32[]{:S(2)}) copy-start(s32[32,512]{1,0:T(8,128)} %param.137) | copy-start | bytes 196612
  1376.8 6.5 collective-permute-start.1
Sparse Core Ops, SparseCore 0:
  16.4 73.9 all-gather.8
  100.4 43.9 all-reduce.6
  151.1 141.5 reduce-scatter.2
  298.6 238.8 all-reduce.8
  563.8 74.1 all-gather.4
  643.9 43.9 all-reduce.10
  694.6 141.5 reduce-scatter.4
  842.3 238.8 all-reduce.12
  1107.5 74.1 all-gather.6
  1187.7 43.9 all-reduce.14
where the time goes:
time: 1400 us; the launch traced here: 1390 us
  waiting for transfers between devices  1040 us (74%)
  other arithmetic  234 us (17%)
  local copies, waits for them, and re-layouts  46 us (3%)
  matrix products  45.7 us (3%)
  between operations  15.6 us (1%)
    psum x2, waiting for transfers between devices, shards(): gram_matrix = lax.psum(local_gram, ('rows', 'coil'))  486 us
    reduce_scatter x2, waiting for transfers between devices, shards(): lax.psum_scatter(lax.dot_general(hankel_cols, images, (((1,), (1,)), ((),...  283 us
    another operation x128, other arithmetic  139 us
    all_gather x2, waiting for transfers between devices, apply_hankel(): lax.all_gather(current, 'rows', axis=0, tiled=True)  102 us
    psum x3, waiting for transfers between devices, coil_total(): return lax.psum(partial_value, 'coil')  89.5 us
    all_gather x1, waiting for transfers between devices, shards(): lax.all_gather(owned_basis, 'rows', axis=0, tiled=True)  74.2 us
    unnamed x63, other arithmetic  45.3 us
    scatter-add x64, local copies, waits for them, and re-layouts, shards(): spread = spread.at[:, offset:offset + tile_rows].add(stacked[offset])  43.2 us
  transfers between devices with their start and end apart: 12, of which 12 were waited for; matrix products, arithmetic and copies ran while one was open for 6% of the time, Pallas kernels for 0%

commit v1 on v0

--- a/solution.py
+++ b/solution.py
@@ -69,7 +69,9 @@
         local_gram = jnp.dot(
             normal_rows.T, normal_rows, precision=highest, preferred_element_type=jnp.float32
         )
-        gram_matrix = lax.psum(local_gram, ("rows", "coil"))
+        gram_matrix = local_gram
+        for mesh_axis in ("rows", "coil"):
+            gram_matrix = lax.psum(gram_matrix, mesh_axis)
         owned_basis = orthonormal(normal_rows, gram_matrix)
     images = apply_hankel(owned_basis)
     projected = jnp.dot(

time: 1400 us -> 1360 us (0.971)
  waiting for transfers between devices: 1040 us -> 995 us
    psum x2 -> x4, waiting for transfers between devices: 486 us -> 431 us  [shards(): gram_matrix = lax.psum(gram_matrix, mesh_axis)]
  transfers between devices with their start and end apart: 12 -> 14, of which waited for: 12 -> 14; matrix products, arithmetic and copies ran while one was open for 6% -> 7% of each run, Pallas kernels for 0% -> 0%
where the time goes in v1:
time: 1360 us; the launch traced here: 1350 us
  waiting for transfers between devices  995 us (73%)
  other arithmetic  234 us (17%)
  local copies, waits for them, and re-layouts  46 us (3%)
  matrix products  45.7 us (3%)
  between operations  15.7 us (1%)
    psum x4, waiting for transfers between devices, shards(): gram_matrix = lax.psum(gram_matrix, mesh_axis)  431 us
    reduce_scatter x2, waiting for transfers between devices, shards(): lax.psum_scatter(lax.dot_general(hankel_cols, images, (((1,), (1,)), ((),...  283 us
    another operation x128, other arithmetic  139 us
    all_gather x2, waiting for transfers between devices, apply_hankel(): lax.all_gather(current, 'rows', axis=0, tiled=True)  106 us
    psum x3, waiting for transfers between devices, coil_total(): return lax.psum(partial_value, 'coil')  89.5 us
    all_gather x1, waiting for transfers between devices, shards(): lax.all_gather(owned_basis, 'rows', axis=0, tiled=True)  78.2 us
    unnamed x63, other arithmetic  45.3 us
    scatter-add x64, local copies, waits for them, and re-layouts, shards(): spread = spread.at[:, offset:offset + tile_rows].add(stacked[offset])  43.2 us
  transfers between devices with their start and end apart: 14, of which 14 were waited for; matrix products, arithmetic and copies ran while one was open for 7% of the time, Pallas kernels for 0%

profile of v1, /device:TPU:16, one launch (start us, length us, event | category | flops | bytes accessed | tf_op | source)
XLA Modules:
  0.0 1345.2 jit_solution(13047322408078931624)
XLA Ops:
  8.7 7.5 collective-permute-start
  62.2 28.1 %all-gather.9.cloned.1.call-done = f32[1,2048,128]{2,1,0:T(8,128)} async-done(((f32[1,32,128]{2,1,0:T(8,128)}), f32[1,2048,128]{2,1,0:T(8,128)}) %all-gather.9.cloned.1.call-update) | async-done | bytes 1048592 | tf_op jit(solution)/shard_map/all_gather | solution.py:52
  90.4 9.9 convolution_bitcast_fusion
  100.5 43.9 %all-reduce.9.cloned.1.call-done = f32[128,512]{0,1:T(8,128)} async-done(((f32[128,512]{0,1:T(8,128)}), f32[128,512]{0,1:T(8,128)}) %all-reduce.9.cloned.1.call-update) | async-done | bytes 262160 | tf_op jit(solution)/shard_map/psum | solution.py:25
  144.4 6.6 fusion.135
  151.0 141.7 %reduce-scatter.3.cloned.1.call-done = f32[32,128]{1,0:T(8,128)} async-done(((f32[2048,128]{1,0:T(8,128)}), f32[32,128]{1,0:T(8,128)}) %reduce-scatter.3.cloned.1.call-update) | async-done | bytes 16400 | tf_op jit(solution)/shard_map/reduce_scatter | solution.py:57
  292.7 1.7 fusion.136
  294.5 170.9 %all-reduce.11.cloned.1.call-done = f32[128,128]{0,1:T(8,128)} async-done(((f32[128,128]{0,1:T(8,128)}), f32[128,128]{0,1:T(8,128)}) %all-reduce.11.cloned.1.call-update) | async-done | bytes 65552 | tf_op jit(solution)/shard_map/psum | solution.py:74
  465.5 44.6 %all-reduce.13.cloned.1.call-done = f32[128,128]{0,1:T(8,128)} async-done(((f32[128,128]{0,1:T(8,128)}), f32[128,128]{0,1:T(8,128)}) %all-reduce.13.cloned.1.call-update) | async-done | bytes 65552 | tf_op jit(solution)/shard_map/psum | solution.py:74
  511.9 11.7 cholesky.44
  524.9 9.8 custom-call.6
  536.5 77.9 %all-gather.5.cloned.1.call-done = f32[2048,128]{1,0:T(8,128)} async-done(((f32[32,128]{1,0:T(8,128)}), f32[2048,128]{1,0:T(8,128)}) %all-gather.5.cloned.1.call-update) | async-done | bytes 1048592 | tf_op jit(solution)/shard_map/all_gather | solution.py:52
  614.5 5.8 fusion.137
  620.4 44.0 %all-reduce.15.cloned.1.call-done = f32[128,512]{1,0:T(8,128)} async-done(((f32[128,512]{1,0:T(8,128)}), f32[128,512]{1,0:T(8,128)}) %all-reduce.15.cloned.1.call-update) | async-done | bytes 262160 | tf_op jit(solution)/shard_map/psum | solution.py:25
  664.4 6.6 fusion.138
  671.1 141.7 %reduce-scatter.5.cloned.1.call-done = f32[32,128]{1,0:T(8,128)} async-done(((f32[2048,128]{1,0:T(8,128)}), f32[32,128]{1,0:T(8,128)}) %reduce-scatter.5.cloned.1.call-update) | async-done | bytes 16400 | tf_op jit(solution)/shard_map/reduce_scatter | solution.py:57
  812.8 1.7 fusion.139
  814.6 171.1 %all-reduce.17.cloned.1.call-done = f32[128,128]{0,1:T(8,128)} async-done(((f32[128,128]{0,1:T(8,128)}), f32[128,128]{0,1:T(8,128)}) %all-reduce.17.cloned.1.call-update) | async-done | bytes 65552 | tf_op jit(solution)/shard_map/psum | solution.py:74
  986.2 44.2 %all-reduce.19.cloned.1.call-done = f32[128,128]{0,1:T(8,128)} async-done(((f32[128,128]{0,1:T(8,128)}), f32[128,128]{0,1:T(8,128)}) %all-reduce.19.cloned.1.call-update) | async-done | bytes 65552 | tf_op jit(solution)/shard_map/psum | solution.py:74
  1032.1 11.7 cholesky.55
  1045.2 9.8 custom-call.7
  1056.6 78.2 %all-gather.7.cloned.1.call-done = f32[2048,128]{1,0:T(8,128)} async-done(((f32[32,128]{1,0:T(8,128)}), f32[2048,128]{1,0:T(8,128)}) %all-gather.7.cloned.1.call-update) | async-done | bytes 1048592 | tf_op jit(solution)/shard_map/all_gather | solution.py:78
  1134.7 5.9 fusion.140
  1183.2 1.6 all-reduce.21.cloned.1.call-done
  1184.8 4.5 fusion.141
  1194.1 1.6 add_select_fusion.59
  1196.3 1.6 add_select_fusion.58
  1205.2 1.6 add_select_fusion.54
  1209.7 1.6 add_select_fusion.52
  1212.0 1.5 add_select_fusion.51
  1214.2 1.6 add_select_fusion.50
  1216.5 1.5 add_select_fusion.49
  1218.7 1.6 add_select_fusion.48
  1223.1 1.6 add_select_fusion.46
  1225.4 1.5 add_select_fusion.45
  1227.6 1.6 add_select_fusion.44
  1232.2 1.6 add_select_fusion.42
  1234.5 1.6 add_select_fusion.41
  1239.0 1.5 add_select_fusion.39
  1241.3 1.5 add_select_fusion.38
  1243.5 1.5 add_select_fusion.37
  1245.7 1.5 add_select_fusion.36
  1248.0 1.6 add_select_fusion.35
  1252.5 1.6 add_select_fusion.33
  1254.8 1.6 add_select_fusion.32
  1257.1 1.6 add_select_fusion.31
  1261.5 1.6 add_select_fusion.29
  1266.0 1.6 add_select_fusion.27
  1272.7 1.6 add_select_fusion.24
  1275.0 1.6 add_select_fusion.23
  1279.5 1.5 add_select_fusion.21
  1281.7 1.5 add_select_fusion.20
  1284.0 1.6 add_select_fusion.19
  1288.4 1.6 add_select_fusion.17
  1292.9 1.6 add_select_fusion.15
  1297.3 1.6 add_select_fusion.13
  1301.8 1.6 add_select_fusion.11
  1304.0 1.5 add_select_fusion.10
  1306.2 1.6 add_select_fusion.9
  1312.9 1.6 add_select_fusion.6
  1317.4 1.6 add_select_fusion.4
  1322.2 1.6 add_select_fusion.2
  1324.4 1.6 add_select_fusion.1
  1331.2 5.2 collective-permute-done.1
  (270 shorter events, 183.5 us)
Async XLA Ops:
  7.2 83.2 %all-gather.9.cloned.1.call-start = ((), (), s32[]{:S(2)}) async-start(), calls=%async_computation.13 | async-start | bytes 1064960 | tf_op jit(solution)/shard_map/all_gather | solution.py:52
  8.7 8.9 collective-permute-start
  16.2 128.1 %all-reduce.9.cloned.1.call-start = ((), (), s32[]{:S(2)}) async-start(), calls=%async_computation.2 | async-start | bytes 524288 | tf_op jit(solution)/shard_map/psum | solution.py:25
  100.3 192.4 %reduce-scatter.3.cloned.1.call-start = ((), (), s32[]{:S(2)}) async-start(), calls=%async_computation.3 | async-start | bytes 1064960 | tf_op jit(solution)/shard_map/reduce_scatter | solution.py:57
  151.0 314.4 %all-reduce.11.cloned.1.call-start = ((), (), s32[]{:S(2)}) async-start(), calls=%async_computation.4 | async-start | bytes 131072 | tf_op jit(solution)/shard_map/psum | solution.py:74
  294.4 215.6 %all-reduce.13.cloned.1.call-start = ((), (), s32[]{:S(2)}) async-start(), calls=%async_computation.5 | async-start | bytes 131072 | tf_op jit(solution)/shard_map/psum | solution.py:74
  465.5 149.0 %all-gather.5.cloned.1.call-start = ((), (), s32[]{:S(2)}) async-start(), calls=%async_computation.6 | async-start | bytes 1064960 | tf_op jit(solution)/shard_map/all_gather | solution.py:52
  536.3 128.1 %all-reduce.15.cloned.1.call-start = ((), (), s32[]{:S(2)}) async-start(), calls=%async_computation.7 | async-start | bytes 524288 | tf_op jit(solution)/shard_map/psum | solution.py:25
  620.3 192.5 %reduce-scatter.5.cloned.1.call-start = ((), (), s32[]{:S(2)}) async-start(), calls=%async_computation.8 | async-start | bytes 1064960 | tf_op jit(solution)/shard_map/reduce_scatter | solution.py:57
  671.0 314.6 %all-reduce.17.cloned.1.call-start = ((), (), s32[]{:S(2)}) async-start(), calls=%async_computation.9 | async-start | bytes 131072 | tf_op jit(solution)/shard_map/psum | solution.py:74
  814.5 215.8 %all-reduce.19.cloned.1.call-start = ((), (), s32[]{:S(2)}) async-start(), calls=%async_computation.10 | async-start | bytes 131072 | tf_op jit(solution)/shard_map/psum | solution.py:74
  985.7 149.0 %all-gather.7.cloned.1.call-start = ((), (), s32[]{:S(2)}) async-start(), calls=%async_computation.11 | async-start | bytes 1064960 | tf_op jit(solution)/shard_map/all_gather | solution.py:78
  1056.5 128.2 %all-reduce.21.cloned.1.call-start = ((), (), s32[]{:S(2)}) async-start(), calls=%async_computation.12 | async-start | bytes 524288 | tf_op jit(solution)/shard_map/psum | solution.py:25
  1134.7 50.0 %copy-start.1 = (f32[2048,128]{1,0:T(8,128)S(1)}, f32[2048,128]{1,0:T(8,128)}, u32[]{:S(2)}) copy-start(f32[2048,128]{1,0:T(8,128)} %all-gather.7.cloned.1.call-done) | copy-start | bytes 3145732
  1189.2 2.0 copy-start
  1275.0 62.4 %copy-start.2 = (f32[32,512]{1,0:T(8,128)S(1)}, f32[32,512]{1,0:T(8,128)}, u32[]{:S(2)}) copy-start(f32[32,512]{1,0:T(8,128)} %param.136) | copy-start | bytes 196612
  1275.0 62.4 %copy-start.3 = (s32[32,512]{1,0:T(8,128)S(1)}, s32[32,512]{1,0:T(8,128)}, u32[]{:S(2)}) copy-start(s32[32,512]{1,0:T(8,128)} %param.137) | copy-start | bytes 196612
  1329.9 6.5 collective-permute-start.1
Sparse Core Ops, SparseCore 0:
  16.4 73.9 all-gather.8
  100.4 43.9 all-reduce.8
  151.1 141.5 reduce-scatter.2
  296.6 168.7 all-reduce.10
  467.6 42.4 all-reduce.12
  536.4 78.0 all-gather.4
  620.4 43.9 all-reduce.14
  671.2 141.5 reduce-scatter.4
  816.8 168.8 all-reduce.16
  987.8 42.4 all-reduce.18
  1056.6 78.0 all-gather.6
  1140.8 43.9 all-reduce.20
